TPU v7x, 256 devices: a whole 4x4x8 slice. The times are simulated.
256 devices in a mesh: tm: 8 (over x_hi, y), azim: 32 (over z, x_lo, core).
Axes of the slice: x: 4 (x_hi: 2, x_lo: 2; x = x_hi * 2 + x_lo), y: 4, z: 8, core: 2. Of those that a mesh axis runs over, the one named last changes fastest.
Arguments:
- rotor_coeffs: float32 [64, 2, 32, 16384], P('tm', None, 'azim'), may hold values from -1.5 to 1.5
- mortar_weights: float32 [64, 2, 32, 16384], P('tm', None, 'azim'), may hold values from 0.2 to 1
- block_shifts: int32 [64], P('tm'), may hold values from 0 to 31
- stencil_offsets: int32 [64, 2], P('tm'), may hold values from -1 to 1
- reluctivity: float32 [32, 16384], P('azim'), may hold values from 0.5 to 2
- source: float32 [64, 2, 32, 16384], P('tm', None, 'azim'), may hold values from -3 to 3
Outputs:
- residual: float32 [64, 2, 32, 16384], P('tm', None, 'azim')
All inputs are finite; a program needn't handle non-finite values.
Results may differ from a plain program's by a relative error of at most 0.0001.
Values sent between devices are 32-bit elements; how exact they have to be, the bound alone decides.
A program may use at most 128 MiB of HBM per device.

v0:
```python
import jax
import jax.numpy as jnp
from jax import lax
from jax.sharding import PartitionSpec as P

KC = 64
NT = 64


def shifted(value, axis, steps):
    count = lax.axis_size(axis)
    pairs = [(source, (source + steps) % count) for source in range(count)]
    return lax.ppermute(value, axis, pairs)


def with_halo(value, sides, width):
    for axis, dim in sides:
        devices, length = (lax.axis_size(axis), value.shape[dim])
        up = [(i, (i + 1) % devices) for i in range(devices)]
        down = [(j, i) for i, j in up]
        last = lax.slice_in_dim(value, length - width, length, axis=dim)
        initial = lax.slice_in_dim(value, 0, width, axis=dim)
        before = lax.ppermute(last, axis, up)
        after = lax.ppermute(initial, axis, down)
        value = jnp.concatenate([before, value, after], axis=dim)
    return value


def harmonic_basis(sample_rows, coefficient_count):
    column = jnp.arange(coefficient_count, dtype=jnp.int32)
    harmonic_order = 2 * (column // 2) + 1
    phase_index = harmonic_order[None, :] * (2 * sample_rows[:, None] + 1) % (4 * NT)
    phase_angle = phase_index.astype(jnp.float32) * (jnp.pi / (2 * NT))
    return jnp.where(column[None, :] % 2 == 0, jnp.cos(phase_angle), jnp.sin(phase_angle))


def body(rotor_coeffs, mortar_weights, block_shifts, stencil_offsets, reluctivity, source):
    sample_rows = mortar_weights.shape[0]
    stencil_count = mortar_weights.shape[1]
    full_table = harmonic_basis(jnp.arange(NT, dtype=jnp.int32), KC)
    spread = jnp.einsum(
        "jc,cabp->jabp",
        full_table,
        lax.all_to_all(rotor_coeffs, "tm", split_axis=3, concat_axis=0, tiled=True),
        precision=lax.Precision.HIGHEST,
    )
    samples = lax.all_to_all(spread, "tm", split_axis=0, concat_axis=3, tiled=True)
    turned = samples
    for bit_level in range((lax.axis_size("azim") - 1).bit_length()):
        moved = shifted(turned, "azim", 1 << bit_level)
        chosen = block_shifts >> bit_level & 1 == 1
        turned = jnp.where(chosen[:, None, None, None], moved, turned)
    padded = with_halo(turned, (("azim", 2),), 1)
    airgap_field = jnp.zeros_like(samples)
    for stencil_entry in range(stencil_count):
        pick_index = stencil_offsets[:, stencil_entry] + 1
        neighbour = jnp.zeros_like(samples)
        for position in range(3):
            neighbour = neighbour + jnp.where(
                (pick_index == position)[:, None, None, None],
                padded[:, :, position : position + 1],
                0.0,
            )
        airgap_field = airgap_field + mortar_weights[:, stencil_entry][:, None] * neighbour
    square = jnp.sum(airgap_field * airgap_field, axis=1, keepdims=True)
    field_flux = reluctivity[None, None] * (1.0 + square / (1.0 + square)) * airgap_field
    first_sample = lax.axis_index("tm") * sample_rows
    local_table = harmonic_basis(first_sample + jnp.arange(sample_rows, dtype=jnp.int32), KC) * (
        2.0 / NT
    )
    summed = lax.psum_scatter(
        jnp.einsum("jc,jabp->cabp", local_table, field_flux, precision=lax.Precision.HIGHEST),
        "tm",
        scatter_dimension=0,
        tiled=True,
    )
    return summed - source


def solution(mesh):
    in_specs = (
        P("tm", None, "azim", None),
        P("tm", None, "azim", None),
        P("tm"),
        P("tm", None),
        P("azim", None),
        P("tm", None, "azim", None),
    )
    out_specs = P("tm", None, "azim", None)
    return jax.shard_map(body, mesh=mesh, in_specs=in_specs, out_specs=out_specs, check_vma=False)
```

profile of v0, /device:TPU:1, one launch (start us, length us, event | category | flops | bytes accessed | tf_op | source)
XLA Modules:
  0.0 525.8 jit_solution(4220196497033002725)
XLA Ops:
  6.5 17.4 %copy.23 = f32[8,2,1,16384]{0,1,2,3:T(2,128)} copy(f32[8,2,1,16384]{3,2,1,0:T(1,128)} %param.6) | data formatting | bytes 2097152 | tf_op args[0]
  23.9 29.0 %reshape.168 = f32[8,1,32768]{2,1,0:T(1,128)} reshape(f32[16384,1,2,8]{3,2,1,0:T(2,128)} %bitcast.44) | data formatting | bytes 2097152
  52.9 7.5 %all-to-all-start = ((f32[8,1,32768]{2,1,0:T(1,128)}), f32[8,1,32768]{2,1,0:T(1,128)S(1)}, u32[]{:S(2)}, u32[]{:S(2)}) async-start(f32[8,1,32768]{2,1,0:T(1,128)} %reshape.168), calls=%async_computation | async-start | bytes 2097152 | tf_op jit(solution)/shard_map/all_to_all | solution.py:44
  60.4 0.2 reduce-scatter.2.cloned.1.call-start
  60.6 13.9 %all-to-all-done = f32[8,1,32768]{2,1,0:T(1,128)S(1)} async-done(((f32[8,1,32768]{2,1,0:T(1,128)}), f32[8,1,32768]{2,1,0:T(1,128)S(1)}, u32[]{:S(2)}, u32[]{:S(2)}) %all-to-all-start) | async-done | bytes 1048608 | tf_op jit(solution)/shard_map/all_to_all | solution.py:44
  74.5 0.5 broadcast.282
  75.0 3.1 reduce.1
  78.2 32.1 %reshape.169 = f32[16384,1,2,8]{3,2,1,0:T(2,128)} reshape(f32[8,32768]{1,0:T(8,128)S(1)} %reduce.1) | data formatting | bytes 2097152
  110.3 20.2 %copy.31 = f32[8,2,1,8,2048]{4,0,3,1,2:T(8,128)S(1)} copy(f32[8,2,1,8,2048]{0,1,4,3,2:T(2,128)} %bitcast.43) | data formatting | bytes 2097152 | tf_op jit(solution)/shard_map/all_to_all | solution.py:44
  130.5 1.3 convolution_bitcast_fusion.1
  131.8 0.8 copy.26
  132.6 21.4 %all_to_all.33 = f32[64,2,1,2048]{3,1,2,0:T(2,128)S(1)} all-to-all(f32[64,2,1,2048]{3,1,2,0:T(2,128)S(1)} %copy.26), channel_id=1, replica_groups=mesh['tm'=8,'azim'=32] {'tm'}, dimensions={0} | all-to-all | bytes 2097152 | tf_op jit(solution)/shard_map/all_to_all | solution.py:47
  154.0 0.6 copy.27
  154.6 2.8 collective-permute-start
  157.4 11.7 %collective-permute-done = f32[8,2,1,16384]{3,0,1,2:T(8,128)S(1)} collective-permute-done((f32[8,2,1,16384]{3,0,1,2:T(8,128)S(1)}, f32[8,2,1,16384]{3,0,1,2:T(8,128)S(1)}, u32[]{:S(2)}, u32[]{:S(2)}) %collective-permute-start) | collective-permute-done | bytes 1048608 | tf_op jit(solution)/shard_map/ppermute | solution.py:13
  169.3 2.5 collective-permute-start.1
  171.8 20.8 %collective-permute-done.1 = f32[8,2,1,16384]{3,0,1,2:T(8,128)S(1)} collective-permute-done((f32[8,2,1,16384]{3,0,1,2:T(8,128)S(1)}, f32[8,2,1,16384]{3,0,1,2:T(8,128)S(1)}, u32[]{:S(2)}, u32[]{:S(2)}) %collective-permute-start.1) | collective-permute-done | bytes 1048608 | tf_op jit(solution)/shard_map/ppermute | solution.py:13
  192.9 3.0 collective-permute-start.2
  195.9 21.3 %collective-permute-done.2 = f32[8,2,1,16384]{3,0,1,2:T(8,128)S(1)} collective-permute-done((f32[8,2,1,16384]{3,0,1,2:T(8,128)S(1)}, f32[8,2,1,16384]{3,0,1,2:T(8,128)S(1)}, u32[]{:S(2)}, u32[]{:S(2)}) %collective-permute-start.2) | collective-permute-done | bytes 1048608 | tf_op jit(solution)/shard_map/ppermute | solution.py:13
  217.3 5.8 %collective-permute-start.3 = (f32[8,2,1,16384]{3,0,1,2:T(8,128)S(1)}, f32[8,2,1,16384]{3,0,1,2:T(8,128)S(1)}, u32[]{:S(2)}, u32[]{:S(2)}) collective-permute-start(f32[8,2,1,16384]{3,0,1,2:T(8,128)S(1)} %broadcast_select_fusion.2), channel_id=1, source_target_pairs={{0,8},{1,9},{2,10},{3,11},{4,12},{5,13},{6,14},{7,15},{8,16},{9,17... | collective-permute-start | bytes 3145736 | tf_op jit(solution)/shard_map/ppermute | solution.py:13
  223.2 42.9 %collective-permute-done.3 = f32[8,2,1,16384]{3,0,1,2:T(8,128)S(1)} collective-permute-done((f32[8,2,1,16384]{3,0,1,2:T(8,128)S(1)}, f32[8,2,1,16384]{3,0,1,2:T(8,128)S(1)}, u32[]{:S(2)}, u32[]{:S(2)}) %collective-permute-start.3) | collective-permute-done | bytes 1048608 | tf_op jit(solution)/shard_map/ppermute | solution.py:13
  266.2 1.4 collective-permute-start.4
  267.8 25.5 %collective-permute-done.4 = f32[8,2,1,16384]{3,0,1,2:T(8,128)S(1)} collective-permute-done((f32[8,2,1,16384]{3,0,1,2:T(8,128)S(1)}, f32[8,2,1,16384]{3,0,1,2:T(8,128)S(1)}, u32[]{:S(2)}, u32[]{:S(2)}) %collective-permute-start.4) | collective-permute-done | bytes 1048608 | tf_op jit(solution)/shard_map/ppermute | solution.py:13
  293.4 3.3 collective-permute-start.6
  296.7 3.6 collective-permute-start.5
  300.3 0.6 copy_bitcast_fusion
  301.0 11.8 %collective-permute-done.6 = f32[8,2,1,16384]{3,0,1,2:T(8,128)} collective-permute-done((f32[8,2,1,16384]{3,0,1,2:T(8,128)S(1)}, f32[8,2,1,16384]{3,0,1,2:T(8,128)}, u32[]{:S(2)}, u32[]{:S(2)}) %collective-permute-start.6) | collective-permute-done | bytes 1048608 | tf_op jit(solution)/shard_map/ppermute | solution.py:24
  312.8 2.2 multiply_reduce_fusion
  315.1 9.2 %convolution_bitcast_fusion = f32[64,2,1,16384]{3,0,1,2:T(8,128)} fusion(f32[8,2,1,16384]{3,0,1,2:T(8,128)S(1)} %get-tuple-element.6, f32[8,16384]{1,0:T(8,128)S(1)} %fusion.4, s32[8]{0:T(128)S(1)} %multiply_add_fusion.2, s32[64]{0:T(128)S(1)} %get-tuple-element.20, pred[64]{0:T(512)(128)(4,1)S(1)} %fusion.44), kind=kOutput, calls=%fused_computation | convolution fusion | flops 201596928 | bytes 9961824 | tf_op jit(solution)/shard_map/jc,jabp->cabp/dot_general | solution.py:72
  324.3 190.7 %reduce-scatter.2.cloned.1.call-done = f32[8,2,1,16384]{3,0,1,2:T(8,128)} async-done(((f32[64,2,1,16384]{3,0,1,2:T(8,128)}), f32[8,2,1,16384]{3,0,1,2:T(8,128)}) %reduce-scatter.2.cloned.1.call-update) | async-done | bytes 1048592 | tf_op jit(solution)/shard_map/reduce_scatter | solution.py:71
  515.1 1.9 copy_subtract_fusion
  516.9 2.0 copy.29
  (24 shorter events, 1.1 us)
Async XLA Ops:
  52.9 21.7 %all-to-all-start = ((f32[8,1,32768]{2,1,0:T(1,128)}), f32[8,1,32768]{2,1,0:T(1,128)S(1)}, u32[]{:S(2)}, u32[]{:S(2)}) async-start(f32[8,1,32768]{2,1,0:T(1,128)} %reshape.168), calls=%async_computation | async-start | bytes 2097152 | tf_op jit(solution)/shard_map/all_to_all | solution.py:44
  60.4 454.7 %reduce-scatter.2.cloned.1.call-start = ((), (), s32[]{:S(2)}) async-start(), calls=%async_computation.3 | async-start | bytes 9437184 | tf_op jit(solution)/shard_map/reduce_scatter | solution.py:71
  110.3 47.1 %copy-start.4 = (s32[8]{0:T(128)S(1)}, s32[8]{0:T(128)}, u32[]{:S(2)}) copy-start(s32[8]{0:T(128)} %param.8) | copy-start | bytes 100
  110.3 157.4 %copy-start.1 = (f32[8,2,1,16384]{3,2,1,0:T(1,128)S(1)}, f32[8,2,1,16384]{3,2,1,0:T(1,128)}, u32[]{:S(2)}) copy-start(f32[8,2,1,16384]{3,2,1,0:T(1,128)} %param.7) | copy-start | bytes 3145732
  130.5 170.4 %copy-start.3 = (s32[8,2]{0,1:T(2,128)S(1)}, s32[8,2]{0,1:T(2,128)}, u32[]{:S(2)}) copy-start(s32[8,2]{0,1:T(2,128)} %param.9) | copy-start | bytes 196
  130.5 184.5 %copy-start.2 = (f32[1,16384]{1,0:T(1,128)S(1)}, f32[1,16384]{1,0:T(1,128)}, u32[]{:S(2)}) copy-start(f32[1,16384]{1,0:T(1,128)} %param.10) | copy-start | bytes 196612
  154.6 14.6 %collective-permute-start = (f32[8,2,1,16384]{3,0,1,2:T(8,128)S(1)}, f32[8,2,1,16384]{3,0,1,2:T(8,128)S(1)}, u32[]{:S(2)}, u32[]{:S(2)}) collective-permute-start(f32[8,2,1,16384]{3,0,1,2:T(8,128)S(1)} %bitcast.45), channel_id=1, source_target_pairs={{0,1},{1,2},{2,3},{3,4},{4,5},{5,6},{6,7},{7,8},{8,9},{9,10},{10,1... | collective-permute-start | bytes 3145736 | tf_op jit(solution)/shard_map/ppermute | solution.py:13
  169.3 23.3 %collective-permute-start.1 = (f32[8,2,1,16384]{3,0,1,2:T(8,128)S(1)}, f32[8,2,1,16384]{3,0,1,2:T(8,128)S(1)}, u32[]{:S(2)}, u32[]{:S(2)}) collective-permute-start(f32[8,2,1,16384]{3,0,1,2:T(8,128)S(1)} %broadcast_select_fusion), channel_id=1, source_target_pairs={{0,2},{1,3},{2,4},{3,5},{4,6},{5,7},{6,8},{7,9},{8,10},{9,11},{10,... | collective-permute-start | bytes 3145736 | tf_op jit(solution)/shard_map/ppermute | solution.py:13
  192.9 24.3 %collective-permute-start.2 = (f32[8,2,1,16384]{3,0,1,2:T(8,128)S(1)}, f32[8,2,1,16384]{3,0,1,2:T(8,128)S(1)}, u32[]{:S(2)}, u32[]{:S(2)}) collective-permute-start(f32[8,2,1,16384]{3,0,1,2:T(8,128)S(1)} %broadcast_select_fusion.1), channel_id=1, source_target_pairs={{0,4},{1,5},{2,6},{3,7},{4,8},{5,9},{6,10},{7,11},{8,12},{9,13},{1... | collective-permute-start | bytes 3145736 | tf_op jit(solution)/shard_map/ppermute | solution.py:13
  217.3 48.7 %collective-permute-start.3 = (f32[8,2,1,16384]{3,0,1,2:T(8,128)S(1)}, f32[8,2,1,16384]{3,0,1,2:T(8,128)S(1)}, u32[]{:S(2)}, u32[]{:S(2)}) collective-permute-start(f32[8,2,1,16384]{3,0,1,2:T(8,128)S(1)} %broadcast_select_fusion.2), channel_id=1, source_target_pairs={{0,8},{1,9},{2,10},{3,11},{4,12},{5,13},{6,14},{7,15},{8,16},{9,17... | collective-permute-start | bytes 3145736 | tf_op jit(solution)/shard_map/ppermute | solution.py:13
  266.2 248.8 %copy-start = (f32[8,2,1,16384]{3,2,1,0:T(1,128)S(1)}, f32[8,2,1,16384]{3,2,1,0:T(1,128)}, u32[]{:S(2)}) copy-start(f32[8,2,1,16384]{3,2,1,0:T(1,128)} %param.11) | copy-start | bytes 3145732
  266.2 27.0 %collective-permute-start.4 = (f32[8,2,1,16384]{3,0,1,2:T(8,128)S(1)}, f32[8,2,1,16384]{3,0,1,2:T(8,128)S(1)}, u32[]{:S(2)}, u32[]{:S(2)}) collective-permute-start(f32[8,2,1,16384]{3,0,1,2:T(8,128)S(1)} %broadcast_select_fusion.3), channel_id=1, source_target_pairs={{0,16},{1,17},{2,18},{3,19},{4,20},{5,21},{6,22},{7,23},{8,24},{9,... | collective-permute-start | bytes 3145736 | tf_op jit(solution)/shard_map/ppermute | solution.py:13
  293.4 19.4 %collective-permute-start.6 = (f32[8,2,1,16384]{3,0,1,2:T(8,128)S(1)}, f32[8,2,1,16384]{3,0,1,2:T(8,128)}, u32[]{:S(2)}, u32[]{:S(2)}) collective-permute-start(f32[8,2,1,16384]{3,0,1,2:T(8,128)S(1)} %broadcast_select_fusion.4), channel_id=1, source_target_pairs={{1,0},{2,1},{3,2},{4,3},{5,4},{6,5},{7,6},{8,7},{9,8},{10,9},{11,1... | collective-permute-start | bytes 3145736 | tf_op jit(solution)/shard_map/ppermute | solution.py:24
  296.7 16.1 %collective-permute-start.5 = (f32[8,2,1,16384]{3,0,1,2:T(8,128)S(1)}, f32[8,2,1,16384]{3,0,1,2:T(8,128)}, u32[]{:S(2)}, u32[]{:S(2)}) collective-permute-start(f32[8,2,1,16384]{3,0,1,2:T(8,128)S(1)} %broadcast_select_fusion.4), channel_id=1, source_target_pairs={{0,1},{1,2},{2,3},{3,4},{4,5},{5,6},{6,7},{7,8},{8,9},{9,10},{10,1... | collective-permute-start | bytes 3145736 | tf_op jit(solution)/shard_map/ppermute | solution.py:23
Sparse Core Ops, SparseCore 0:
  324.5 190.5 reduce-scatter.1
where the time goes:
time: 528 us; the launch traced here: 526 us
  waiting for transfers between devices  339 us (64%)
  local copies, waits for them, and re-layouts  103 us (20%)
  starting transfers between devices  30.2 us (6%)
  blocking collectives  21.4 us (4%)
  between operations  13.5 us (3%)
  matrix products  10.4 us (2%)
  other arithmetic  8.16 us (2%)
    reduce_scatter x1, waiting for transfers between devices, body(): lax.psum_scatter(jnp.einsum('jc,jabp->cabp', local_table, field_flux, pre...  191 us
    ppermute x5, waiting for transfers between devices, shifted(): return lax.ppermute(value, axis, pairs)  122 us
    unnamed x14, local copies, waits for them, and re-layouts  79.1 us
    all_to_all x1, blocking collectives, body(): lax.all_to_all(spread, 'tm', split_axis=0, concat_axis=3, tiled=True)  21.4 us
    all_to_all x2, local copies, waits for them, and re-layouts, body(): lax.all_to_all(rotor_coeffs, 'tm', split_axis=3, concat_axis=0, tiled=True)  20.7 us
    ppermute x5, starting transfers between devices, shifted(): return lax.ppermute(value, axis, pairs)  15.6 us
    all_to_all x1, waiting for transfers between devices, body(): lax.all_to_all(rotor_coeffs, 'tm', split_axis=3, concat_axis=0, tiled=True)  13.9 us
    ppermute x1, waiting for transfers between devices, with_halo(): after = lax.ppermute(initial, axis, down)  11.8 us
  transfers between devices with their start and end apart: 9, of which 8 were waited for; matrix products, arithmetic and copies ran while one was open for 0% of the time, Pallas kernels for 0%

commit v1 on v0

--- a/solution.py
+++ b/solution.py
@@ -5,6 +5,13 @@
 
 KC = 64
 NT = 64
+
+
+def exchange_blocks(array, mesh_axis, split, join):
+    size = lax.axis_size(mesh_axis)
+    parts = jnp.stack(jnp.split(array, size, axis=split), axis=0)
+    parts = lax.all_to_all(parts, mesh_axis, split_axis=0, concat_axis=0)
+    return jnp.concatenate(parts, axis=join)
 
 
 def shifted(value, axis, steps):
@@ -41,7 +48,7 @@
     spread = jnp.einsum(
         "jc,cabp->jabp",
         full_table,
-        lax.all_to_all(rotor_coeffs, "tm", split_axis=3, concat_axis=0, tiled=True),
+        exchange_blocks(rotor_coeffs, "tm", 3, 0),
         precision=lax.Precision.HIGHEST,
     )
     samples = lax.all_to_all(spread, "tm", split_axis=0, concat_axis=3, tiled=True)

time: 528 us -> 436 us (0.83)
  local copies, waits for them, and re-layouts: 103 us -> 16.7 us
    unnamed x14 -> x18, local copies, waits for them, and re-layouts: 79.1 us -> 11.6 us
    reduce_scatter x1, waiting for transfers between devices: 191 us -> 169 us  [body(): lax.psum_scatter(jnp.einsum('jc,jabp->cabp', local_table, field_flux, pre...]
    ppermute x1, waiting for transfers between devices: 0.01 us -> 20.9 us  [with_halo(): before = lax.ppermute(last, axis, up)]
    all_to_all x2 -> x0, local copies, waits for them, and re-layouts: 20.7 us -> none  [body(): lax.all_to_all(rotor_coeffs, 'tm', split_axis=3, concat_axis=0, tiled=True)]
  transfers between devices with their start and end apart: 9 -> 9, of which waited for: 8 -> 9; matrix products, arithmetic and copies ran while one was open for 0% -> 0% of each run, Pallas kernels for 0% -> 0%
where the time goes in v1:
time: 436 us; the launch traced here: 435 us
  waiting for transfers between devices  339 us (78%)
  starting transfers between devices  29.4 us (7%)
  blocking collectives  21.5 us (5%)
  local copies, waits for them, and re-layouts  16.7 us (4%)
  between operations  13.5 us (3%)
  matrix products  10.9 us (2%)
  other arithmetic  4.71 us (1%)
    reduce_scatter x1, waiting for transfers between devices, body(): lax.psum_scatter(jnp.einsum('jc,jabp->cabp', local_table, field_flux, pre...  169 us
    ppermute x5, waiting for transfers between devices, shifted(): return lax.ppermute(value, axis, pairs)  123 us
    all_to_all x1, blocking collectives, body(): lax.all_to_all(spread, 'tm', split_axis=0, concat_axis=3, tiled=True)  21.5 us
    ppermute x1, waiting for transfers between devices, with_halo(): before = lax.ppermute(last, axis, up)  20.9 us
    ppermute x5, starting transfers between devices, shifted(): return lax.ppermute(value, axis, pairs)  15.3 us
    all_to_all x1, waiting for transfers between devices, exchange_blocks(): parts = lax.all_to_all(parts, mesh_axis, split_axis=0, concat_axis=0)  14.1 us
    unnamed x18, local copies, waits for them, and re-layouts  11.6 us
    ppermute x1, waiting for transfers between devices, with_halo(): after = lax.ppermute(initial, axis, down)  11.6 us
  transfers between devices with their start and end apart: 9, of which 9 were waited for; matrix products, arithmetic and copies ran while one was open for 0% of the time, Pallas kernels for 0%

profile of v1, /device:TPU:1, one launch (start us, length us, event | category | flops | bytes accessed | tf_op | source)
XLA Modules:
  0.0 435.4 jit_solution(369877964588462634)
XLA Ops:
  6.5 1.6 bitcast_dynamic-update-slice_fusion.7
  8.1 1.6 bitcast_dynamic-update-slice_fusion.6
  9.7 1.6 bitcast_dynamic-update-slice_fusion.5
  11.3 1.6 bitcast_dynamic-update-slice_fusion.4
  12.8 1.6 bitcast_dynamic-update-slice_fusion.3
  14.4 1.6 bitcast_dynamic-update-slice_fusion.2
  16.0 1.6 bitcast_dynamic-update-slice_fusion.1
  17.5 1.6 bitcast_dynamic-update-slice_fusion
  19.1 7.5 %all-to-all-start = ((f32[8,8,2,1,2048]{4,3,2,1,0:T(1,128)}), f32[8,8,2,1,2048]{4,3,2,1,0:T(1,128)S(1)}, u32[]{:S(2)}, u32[]{:S(2)}) async-start(f32[8,8,2,1,2048]{4,3,2,1,0:T(1,128)} %bitcast_dynamic-update-slice_fusion), calls=%async_computation | async-start | bytes 2097152 | tf_op jit(solution)/shard_map/all_to_all | solution.py:13
  26.6 14.1 %all-to-all-done = f32[8,8,2,1,2048]{4,3,2,1,0:T(1,128)S(1)} async-done(((f32[8,8,2,1,2048]{4,3,2,1,0:T(1,128)}), f32[8,8,2,1,2048]{4,3,2,1,0:T(1,128)S(1)}, u32[]{:S(2)}, u32[]{:S(2)}) %all-to-all-start) | async-done | bytes 1048608 | tf_op jit(solution)/shard_map/all_to_all | solution.py:13
  40.8 1.8 convolution_bitcast_fusion.1
  42.5 0.8 copy.11
  43.4 21.5 %all_to_all.23 = f32[64,2,1,2048]{3,1,2,0:T(2,128)S(1)} all-to-all(f32[64,2,1,2048]{3,1,2,0:T(2,128)S(1)} %copy.11), channel_id=1, replica_groups=mesh['tm'=8,'azim'=32] {'tm'}, dimensions={0} | all-to-all | bytes 2097152 | tf_op jit(solution)/shard_map/all_to_all | solution.py:54
  65.5 2.8 collective-permute-start
  68.3 11.7 %collective-permute-done = f32[8,2,1,16384]{3,0,1,2:T(8,128)S(1)} collective-permute-done((f32[8,2,1,16384]{3,0,1,2:T(8,128)S(1)}, f32[8,2,1,16384]{3,0,1,2:T(8,128)S(1)}, u32[]{:S(2)}, u32[]{:S(2)}) %collective-permute-start) | collective-permute-done | bytes 1048608 | tf_op jit(solution)/shard_map/ppermute | solution.py:20
  80.2 2.5 collective-permute-start.1
  82.7 20.8 %collective-permute-done.1 = f32[8,2,1,16384]{3,0,1,2:T(8,128)S(1)} collective-permute-done((f32[8,2,1,16384]{3,0,1,2:T(8,128)S(1)}, f32[8,2,1,16384]{3,0,1,2:T(8,128)S(1)}, u32[]{:S(2)}, u32[]{:S(2)}) %collective-permute-start.1) | collective-permute-done | bytes 1048608 | tf_op jit(solution)/shard_map/ppermute | solution.py:20
  103.7 3.0 collective-permute-start.2
  106.7 21.3 %collective-permute-done.2 = f32[8,2,1,16384]{3,0,1,2:T(8,128)S(1)} collective-permute-done((f32[8,2,1,16384]{3,0,1,2:T(8,128)S(1)}, f32[8,2,1,16384]{3,0,1,2:T(8,128)S(1)}, u32[]{:S(2)}, u32[]{:S(2)}) %collective-permute-start.2) | collective-permute-done | bytes 1048608 | tf_op jit(solution)/shard_map/ppermute | solution.py:20
  128.2 5.8 %collective-permute-start.3 = (f32[8,2,1,16384]{3,0,1,2:T(8,128)S(1)}, f32[8,2,1,16384]{3,0,1,2:T(8,128)S(1)}, u32[]{:S(2)}, u32[]{:S(2)}) collective-permute-start(f32[8,2,1,16384]{3,0,1,2:T(8,128)S(1)} %broadcast_select_fusion.2), channel_id=1, source_target_pairs={{0,8},{1,9},{2,10},{3,11},{4,12},{5,13},{6,14},{7,15},{8,16},{9,17... | collective-permute-start | bytes 3145736 | tf_op jit(solution)/shard_map/ppermute | solution.py:20
  134.1 42.9 %collective-permute-done.3 = f32[8,2,1,16384]{3,0,1,2:T(8,128)S(1)} collective-permute-done((f32[8,2,1,16384]{3,0,1,2:T(8,128)S(1)}, f32[8,2,1,16384]{3,0,1,2:T(8,128)S(1)}, u32[]{:S(2)}, u32[]{:S(2)}) %collective-permute-start.3) | collective-permute-done | bytes 1048608 | tf_op jit(solution)/shard_map/ppermute | solution.py:20
  177.2 1.2 collective-permute-start.4
  178.4 25.9 %collective-permute-done.4 = f32[8,2,1,16384]{3,0,1,2:T(8,128)S(1)} collective-permute-done((f32[8,2,1,16384]{3,0,1,2:T(8,128)S(1)}, f32[8,2,1,16384]{3,0,1,2:T(8,128)S(1)}, u32[]{:S(2)}, u32[]{:S(2)}) %collective-permute-start.4) | collective-permute-done | bytes 1048608 | tf_op jit(solution)/shard_map/ppermute | solution.py:20
  204.5 3.0 collective-permute-start.6
  207.6 3.6 collective-permute-start.5
  211.8 11.6 %collective-permute-done.6 = f32[8,2,1,16384]{3,0,1,2:T(8,128)S(1)} collective-permute-done((f32[8,2,1,16384]{3,0,1,2:T(8,128)S(1)}, f32[8,2,1,16384]{3,0,1,2:T(8,128)S(1)}, u32[]{:S(2)}, u32[]{:S(2)}) %collective-permute-start.6) | collective-permute-done | bytes 1048608 | tf_op jit(solution)/shard_map/ppermute | solution.py:31
  223.3 20.9 %collective-permute-done.5 = f32[8,2,1,16384]{3,0,1,2:T(8,128)} collective-permute-done((f32[8,2,1,16384]{3,0,1,2:T(8,128)S(1)}, f32[8,2,1,16384]{3,0,1,2:T(8,128)}, u32[]{:S(2)}, u32[]{:S(2)}) %collective-permute-start.5) | collective-permute-done | bytes 1048608 | tf_op jit(solution)/shard_map/ppermute | solution.py:30
  244.2 1.9 multiply_reduce_fusion
  246.2 9.2 %convolution_bitcast_fusion = f32[64,2,1,16384]{3,0,1,2:T(8,128)} fusion(f32[8,2,1,16384]{3,0,1,2:T(8,128)S(1)} %get-tuple-element.6, f32[8,16384]{1,0:T(8,128)S(1)} %fusion.5, s32[8]{0:T(128)S(1)} %multiply_add_fusion.2, s32[64]{0:T(128)S(1)} %get-tuple-element.20, pred[64]{0:T(512)(128)(4,1)S(1)} %fusion.45), kind=kOutput, calls=%fused_computation | convolution fusion | flops 201596928 | bytes 9961824 | tf_op jit(solution)/shard_map/jc,jabp->cabp/dot_general | solution.py:79
  255.4 169.3 %reduce-scatter.2.cloned.1.call-done = f32[8,2,1,16384]{3,0,1,2:T(8,128)} async-done(((f32[64,2,1,16384]{3,0,1,2:T(8,128)}), f32[8,2,1,16384]{3,0,1,2:T(8,128)}) %reduce-scatter.2.cloned.1.call-update) | async-done | bytes 1048592 | tf_op jit(solution)/shard_map/reduce_scatter | solution.py:78
  424.7 1.9 copy_subtract_fusion
  426.5 2.0 copy.14
  (26 shorter events, 2.4 us)
Async XLA Ops:
  6.5 61.8 %copy-start.4 = (s32[8]{0:T(128)S(1)}, s32[8]{0:T(128)}, u32[]{:S(2)}) copy-start(s32[8]{0:T(128)} %param.8) | copy-start | bytes 100
  19.1 21.7 %all-to-all-start = ((f32[8,8,2,1,2048]{4,3,2,1,0:T(1,128)}), f32[8,8,2,1,2048]{4,3,2,1,0:T(1,128)S(1)}, u32[]{:S(2)}, u32[]{:S(2)}) async-start(f32[8,8,2,1,2048]{4,3,2,1,0:T(1,128)} %bitcast_dynamic-update-slice_fusion), calls=%async_computation | async-start | bytes 2097152 | tf_op jit(solution)/shard_map/all_to_all | solution.py:13
  26.6 398.1 %reduce-scatter.2.cloned.1.call-start = ((), (), s32[]{:S(2)}) async-start(), calls=%async_computation.3 | async-start | bytes 9437184 | tf_op jit(solution)/shard_map/reduce_scatter | solution.py:78
  43.4 135.0 %copy-start.1 = (f32[8,2,1,16384]{3,2,1,0:T(1,128)S(1)}, f32[8,2,1,16384]{3,2,1,0:T(1,128)}, u32[]{:S(2)}) copy-start(f32[8,2,1,16384]{3,2,1,0:T(1,128)} %param.7) | copy-start | bytes 3145732
  65.5 14.6 %collective-permute-start = (f32[8,2,1,16384]{3,0,1,2:T(8,128)S(1)}, f32[8,2,1,16384]{3,0,1,2:T(8,128)S(1)}, u32[]{:S(2)}, u32[]{:S(2)}) collective-permute-start(f32[8,2,1,16384]{3,0,1,2:T(8,128)S(1)} %bitcast.53), channel_id=1, source_target_pairs={{0,1},{1,2},{2,3},{3,4},{4,5},{5,6},{6,7},{7,8},{8,9},{9,10},{10,1... | collective-permute-start | bytes 3145736 | tf_op jit(solution)/shard_map/ppermute | solution.py:20
  80.2 23.3 %collective-permute-start.1 = (f32[8,2,1,16384]{3,0,1,2:T(8,128)S(1)}, f32[8,2,1,16384]{3,0,1,2:T(8,128)S(1)}, u32[]{:S(2)}, u32[]{:S(2)}) collective-permute-start(f32[8,2,1,16384]{3,0,1,2:T(8,128)S(1)} %broadcast_select_fusion), channel_id=1, source_target_pairs={{0,2},{1,3},{2,4},{3,5},{4,6},{5,7},{6,8},{7,9},{8,10},{9,11},{10,... | collective-permute-start | bytes 3145736 | tf_op jit(solution)/shard_map/ppermute | solution.py:20
  103.6 108.2 %copy-start.3 = (s32[8,2]{0,1:T(2,128)S(1)}, s32[8,2]{0,1:T(2,128)}, u32[]{:S(2)}) copy-start(s32[8,2]{0,1:T(2,128)} %param.9) | copy-start | bytes 196
  103.7 24.3 %collective-permute-start.2 = (f32[8,2,1,16384]{3,0,1,2:T(8,128)S(1)}, f32[8,2,1,16384]{3,0,1,2:T(8,128)S(1)}, u32[]{:S(2)}, u32[]{:S(2)}) collective-permute-start(f32[8,2,1,16384]{3,0,1,2:T(8,128)S(1)} %broadcast_select_fusion.1), channel_id=1, source_target_pairs={{0,4},{1,5},{2,6},{3,7},{4,8},{5,9},{6,10},{7,11},{8,12},{9,13},{1... | collective-permute-start | bytes 3145736 | tf_op jit(solution)/shard_map/ppermute | solution.py:20
  128.2 117.9 %copy-start.2 = (f32[1,16384]{1,0:T(1,128)S(1)}, f32[1,16384]{1,0:T(1,128)}, u32[]{:S(2)}) copy-start(f32[1,16384]{1,0:T(1,128)} %param.10) | copy-start | bytes 196612
  128.2 48.8 %collective-permute-start.3 = (f32[8,2,1,16384]{3,0,1,2:T(8,128)S(1)}, f32[8,2,1,16384]{3,0,1,2:T(8,128)S(1)}, u32[]{:S(2)}, u32[]{:S(2)}) collective-permute-start(f32[8,2,1,16384]{3,0,1,2:T(8,128)S(1)} %broadcast_select_fusion.2), channel_id=1, source_target_pairs={{0,8},{1,9},{2,10},{3,11},{4,12},{5,13},{6,14},{7,15},{8,16},{9,17... | collective-permute-start | bytes 3145736 | tf_op jit(solution)/shard_map/ppermute | solution.py:20
  177.2 27.2 %collective-permute-start.4 = (f32[8,2,1,16384]{3,0,1,2:T(8,128)S(1)}, f32[8,2,1,16384]{3,0,1,2:T(8,128)S(1)}, u32[]{:S(2)}, u32[]{:S(2)}) collective-permute-start(f32[8,2,1,16384]{3,0,1,2:T(8,128)S(1)} %broadcast_select_fusion.3), channel_id=1, source_target_pairs={{0,16},{1,17},{2,18},{3,19},{4,20},{5,21},{6,22},{7,23},{8,24},{9,... | collective-permute-start | bytes 3145736 | tf_op jit(solution)/shard_map/ppermute | solution.py:20
  204.5 18.8 %collective-permute-start.6 = (f32[8,2,1,16384]{3,0,1,2:T(8,128)S(1)}, f32[8,2,1,16384]{3,0,1,2:T(8,128)S(1)}, u32[]{:S(2)}, u32[]{:S(2)}) collective-permute-start(f32[8,2,1,16384]{3,0,1,2:T(8,128)S(1)} %broadcast_select_fusion.4), channel_id=1, source_target_pairs={{1,0},{2,1},{3,2},{4,3},{5,4},{6,5},{7,6},{8,7},{9,8},{10,9},{11,1... | collective-permute-start | bytes 3145736 | tf_op jit(solution)/shard_map/ppermute | solution.py:31
  207.6 36.6 %collective-permute-start.5 = (f32[8,2,1,16384]{3,0,1,2:T(8,128)S(1)}, f32[8,2,1,16384]{3,0,1,2:T(8,128)}, u32[]{:S(2)}, u32[]{:S(2)}) collective-permute-start(f32[8,2,1,16384]{3,0,1,2:T(8,128)S(1)} %broadcast_select_fusion.4), channel_id=1, source_target_pairs={{0,1},{1,2},{2,3},{3,4},{4,5},{5,6},{6,7},{7,8},{8,9},{9,10},{10,1... | collective-permute-start | bytes 3145736 | tf_op jit(solution)/shard_map/ppermute | solution.py:30
  246.2 178.5 %copy-start = (f32[8,2,1,16384]{3,2,1,0:T(1,128)S(1)}, f32[8,2,1,16384]{3,2,1,0:T(1,128)}, u32[]{:S(2)}) copy-start(f32[8,2,1,16384]{3,2,1,0:T(1,128)} %param.11) | copy-start | bytes 3145732
Sparse Core Ops, SparseCore 0:
  255.5 169.1 reduce-scatter.1
